TPU v7x, 128 devices: a whole 4x4x4 slice. The times are simulated.
128 devices in a mesh: dp: 16 (over x, z), tensor: 8 (over y, core).
Axes of the slice: x: 4, y: 4, z: 4, core: 2. Of those that a mesh axis runs over, the one named last changes fastest.
Arguments:
- attn_out: bfloat16 [8192, 8192], P('dp', 'tensor'), may hold values from -6 to 6
- frozen_weight: bfloat16 [8192, 8192], P('tensor', 'dp'), may hold values from -0.0625 to 0.0625
- vector_bank: float32 [256, 256], replicated, may hold values from -0.18 to 0.18
- logits_a: float32 [16, 32, 2], P(None, 'tensor'), may hold values from -2 to 2
- index_a: int32 [16, 32, 2], P(None, 'tensor'), may hold values from 0 to 255, all different within a row
- logits_b: float32 [16, 32, 2], P(None, 'tensor'), may hold values from -2 to 2
- index_b: int32 [16, 32, 2], P(None, 'tensor'), may hold values from 0 to 255, all different within a row
- out_grad: bfloat16 [8192, 8192], P('dp'), may hold values from -6 to 6
Outputs:
- layer_out: bfloat16 [8192, 8192], P('dp', 'tensor')
- attn_grad: bfloat16 [8192, 8192], P('dp', 'tensor')
- bank_grad: float32 [256, 256], replicated
- logits_a_grad: float32 [16, 32, 2], P(None, 'tensor')
- logits_b_grad: float32 [16, 32, 2], P(None, 'tensor')
Inputs may be any that keep to these rules, and one draw needn't show every extreme that they name: `index_a`: the 2 entries of one sub-vector differ. `index_b`: the 2 entries of one sub-vector differ.
All inputs are finite; a program needn't handle non-finite values.
Results may differ from a plain program's by a relative error of at most 0.014.
Values may be sent and summed in bfloat16 or wider, within the bound.
No kernel may reach another device: no remote copies, remote signals or barrier semaphores. Data moves between devices by JAX's collectives and lax.ppermute only.
A program may use at most 128 MiB of HBM per device.

v0:
```python
import jax
import jax.numpy as jnp
from jax import lax
from jax.sharding import PartitionSpec as P

adapter_scale = 2.0


def from_everyone(x, axis):
    copies = jnp.broadcast_to(x, (lax.axis_size(axis), *x.shape))
    return lax.all_to_all(copies, axis, split_axis=0, concat_axis=0, tiled=True)


def over_copies(x, axis):
    everything = from_everyone(x, axis)
    return jnp.sum(everything, axis=0)


def packed_total(arrays, axis):
    ends = [0]
    for a in arrays:
        ends.append(ends[-1] + a.size)
    running = over_copies(jnp.concatenate([a.ravel() for a in arrays]), axis)
    return tuple((running[b:e].reshape(a.shape) for a, b, e in zip(arrays, ends, ends[1:])))


def gathered_total(x, axis):
    parts = lax.all_gather(x, axis)
    return parts.sum(axis=0)


def compose(logits, indices, vector_bank):
    weights = jax.nn.sigmoid(logits - logits[..., ::-1])
    levels = jnp.arange(vector_bank.shape[0], dtype=jnp.int32)
    picked = (indices[..., None] == levels).astype(jnp.float32)
    mixing = jnp.sum(picked * weights[..., None], axis=2)
    blocks = jnp.einsum("rjb,bc->rjc", mixing, vector_bank, precision=lax.Precision.HIGHEST)
    return (weights, picked, mixing, blocks.reshape(blocks.shape[0], -1))


def compose_back(grad_rows, weights, picked, mixing, vector_bank):
    blocks = grad_rows.reshape(mixing.shape[0], mixing.shape[1], -1)
    bank_part = jnp.einsum("rjb,rjc->bc", mixing, blocks, precision=lax.Precision.HIGHEST)
    projected = jnp.einsum("rjc,bc->rjb", blocks, vector_bank, precision=lax.Precision.HIGHEST)
    dots = jnp.sum(picked * projected[:, :, None, :], axis=3)
    logit_grad = weights * (dots - jnp.sum(weights * dots, axis=2, keepdims=True))
    return (bank_part, logit_grad)


def local(attn_out, frozen_weight, vector_bank, logits_a, index_a, logits_b, index_b, out_grad):
    weights_a, picked_a, mixing_a, rows_a = compose(logits_a, index_a, vector_bank)
    weights_b, picked_b, mixing_b, rows_b = compose(logits_b, index_b, vector_bank)
    down_a = rows_a.astype(jnp.bfloat16)
    up_b = rows_b.astype(jnp.bfloat16)
    own_width = up_b.shape[1]
    grad_cols = lax.dynamic_slice_in_dim(
        out_grad, lax.axis_index("tensor") * own_width, own_width, 1
    )
    low_part = jnp.dot(attn_out, down_a.T, preferred_element_type=jnp.float32)
    back_part = jnp.dot(grad_cols, up_b.T, preferred_element_type=jnp.float32)
    low_total, back_total = packed_total((low_part, back_part), "tensor")
    low_bf = low_total.astype(jnp.bfloat16)
    gathered = lax.all_gather(frozen_weight, "dp", axis=1, tiled=True)
    partial_value = jnp.dot(attn_out, gathered, preferred_element_type=jnp.float32).astype(
        jnp.bfloat16
    )
    summed = lax.psum_scatter(partial_value, "tensor", scatter_dimension=1, tiled=True).astype(
        jnp.float32
    )
    layer_out = (
        summed + adapter_scale * jnp.dot(low_bf, up_b, preferred_element_type=jnp.float32)
    ).astype(jnp.bfloat16)
    back_bf = back_total.astype(jnp.bfloat16)
    main = lax.dot_general(
        out_grad, gathered, (((1,), (1,)), ((), ())), preferred_element_type=jnp.float32
    )
    attn_grad = (
        main + adapter_scale * jnp.dot(back_bf, down_a, preferred_element_type=jnp.float32)
    ).astype(jnp.bfloat16)
    factor = adapter_scale / (attn_out.shape[0] * lax.axis_size("dp"))
    grad_a = factor * lax.dot_general(
        back_bf, attn_out, (((0,), (0,)), ((), ())), preferred_element_type=jnp.float32
    )
    grad_b = factor * lax.dot_general(
        low_bf, grad_cols, (((0,), (0,)), ((), ())), preferred_element_type=jnp.float32
    )
    bank_a, logit_grad_a = compose_back(grad_a, weights_a, picked_a, mixing_a, vector_bank)
    bank_b, logit_grad_b = compose_back(grad_b, weights_b, picked_b, mixing_b, vector_bank)
    bank_part = bank_a + bank_b
    bank_group = over_copies(bank_part, "tensor")
    bank_grad, logits_a_grad, logits_b_grad = (
        gathered_total(bank_group, "dp"),
        gathered_total(logit_grad_a, "dp"),
        gathered_total(logit_grad_b, "dp"),
    )
    return (layer_out, attn_grad, bank_grad, logits_a_grad, logits_b_grad)


def solution(mesh):
    return jax.shard_map(
        local,
        mesh=mesh,
        in_specs=(
            P("dp", "tensor"),
            P("tensor", "dp"),
            P(),
            P(None, "tensor", None),
            P(None, "tensor", None),
            P(None, "tensor", None),
            P(None, "tensor", None),
            P("dp", None),
        ),
        out_specs=(
            P("dp", "tensor"),
            P("dp", "tensor"),
            P(),
            P(None, "tensor", None),
            P(None, "tensor", None),
        ),
        check_vma=False,
    )
```

profile of v0, /device:TPU:1, one launch (start us, length us, event | category | flops | bytes accessed | tf_op | source)
XLA Modules:
  0.0 252.0 jit_solution(6651424941803468780)
XLA Ops:
  7.2 0.7 all-gather.6.cloned.1.call-update
  8.0 0.7 rev.7
  8.7 0.7 add_divide_fusion
  9.4 0.8 select_reduce_fusion.2
  10.2 1.2 fusion.2
  11.4 1.6 fusion.4
  13.2 0.7 rev.6
  13.9 0.7 add_divide_fusion.1
  14.6 0.8 select_reduce_fusion.3
  15.4 1.2 fusion.1
  16.6 0.4 convolution_bitcast_fusion.2
  17.6 15.2 %all_to_all.11 = f32[8,1,16384]{2,1,0:T(1,128)S(1)} all-to-all(f32[8,1,16384]{2,1,0:T(1,128)S(1)} %broadcast_in_dim.4), channel_id=1, replica_groups=mesh['dp'=16,'tensor'=8] {'tensor'}, dimensions={0} | all-to-all | bytes 1048576 | tf_op jit(solution)/shard_map/all_to_all | solution.py:11
  32.8 0.5 reduce_sum.101
  33.5 1.5 convolution_multiply_fusion
  35.1 0.4 convolution_bitcast_fusion
  35.8 0.4 fusion
  36.4 30.0 %all_to_all.12 = f32[8,256,256]{2,1,0:T(8,128)S(1)} all-to-all(f32[8,256,256]{2,1,0:T(8,128)S(1)} %broadcast_in_dim.5), channel_id=1, replica_groups=mesh['dp'=16,'tensor'=8] {'tensor'}, dimensions={0} | all-to-all | bytes 4194304 | tf_op jit(solution)/shard_map/all_to_all | solution.py:11
  66.3 0.8 reduce_sum.102
  67.2 66.4 %all-gather.6.cloned.1.call-done = bf16[1024,8192]{1,0:T(8,128)(2,1)} async-done(((bf16[1024,512]{1,0:T(8,128)(2,1)}), bf16[1024,8192]{1,0:T(8,128)(2,1)}) %all-gather.6.cloned.1.call-update) | async-done | bytes 16777232 | tf_op jit(solution)/shard_map/all_gather | solution.py:63
  133.7 16.8 %convolution_convert_fusion = bf16[512,8192]{1,0:T(8,128)(2,1)} fusion(bf16[512,1024]{1,0:T(8,128)(2,1)S(1)} %copy-done, bf16[1024,8192]{1,0:T(8,128)(2,1)} %all-gather.6.cloned.1.call-done), kind=kOutput, calls=%fused_computation | convolution fusion | flops 8594128896 | bytes 26214400 | tf_op jit(solution)/shard_map/dot_general | solution.py:64
  150.5 0.9 copy-done.1
  151.4 0.4 fusion.8
  152.1 17.9 %all-gather.1 = f32[256,4,2]{1,2,0:T(2,128)S(1)} all-gather(f32[16,4,2]{1,2,0:T(2,128)S(1)} %copy.95), channel_id=3, replica_groups=mesh['dp'=16,'tensor'=8] {'dp'}, dimensions={0}, use_global_device_ids=true | all-gather | bytes 8704 | tf_op jit(solution)/shard_map/all_gather | solution.py:28
  170.1 0.7 copy.98
  170.8 0.4 fusion.6
  171.5 19.0 %all-gather.2 = f32[256,4,2]{1,2,0:T(2,128)S(1)} all-gather(f32[16,4,2]{1,2,0:T(2,128)S(1)} %copy.97), channel_id=4, replica_groups=mesh['dp'=16,'tensor'=8] {'dp'}, dimensions={0}, use_global_device_ids=true | all-gather | bytes 8704 | tf_op jit(solution)/shard_map/all_gather | solution.py:28
  190.6 0.7 copy.99
  191.3 0.4 fusion.23
  191.7 3.2 %reduce_sum.103 = f32[256,256]{1,0:T(8,128)} reduce(f32[16,256,256]{2,1,0:T(8,128)} %bitcast.56, f32[]{:T(128)} %constant.5.clone.1), dimensions={0}, to_apply=%region_5.0 | reduce | flops 983040 | bytes 4456452 | tf_op jit(solution)/shard_map/reduce_sum | solution.py:29
  194.9 16.3 %add_convert_fusion = bf16[512,1024]{1,0:T(8,128)(2,1)} fusion(f32[512,1024]{1,0:T(8,128)S(1)} %fusion.23, bf16[512,8192]{1,0:T(8,128)(2,1)} %param.15, bf16[1024,8192]{1,0:T(8,128)(2,1)} %all-gather.6.cloned.1.call-done), kind=kOutput, calls=%fused_computation.1 | convolution fusion | flops 8591507456 | bytes 28311552 | tf_op jit(solution)/shard_map/dot_general | solution.py:74
  211.2 31.6 %reduce-scatter.2.cloned.1.call-done = bf16[512,1024]{1,0:T(8,128)(2,1)} async-done(((bf16[512,8192]{1,0:T(8,128)(2,1)}), bf16[512,1024]{1,0:T(8,128)(2,1)}) %reduce-scatter.2.cloned.1.call-update) | async-done | bytes 1048592 | tf_op jit(solution)/shard_map/reduce_scatter | solution.py:67
  242.9 2.6 %add_convert_fusion.1 = bf16[512,1024]{1,0:T(8,128)(2,1)} fusion(bf16[512,1024]{1,0:T(8,128)(2,1)} %reduce-scatter.2.cloned.1.call-done, bf16[512,16]{1,0:T(8,128)(2,1)S(1)} %convert_element_type.40, bf16[16,1024]{1,0:T(8,128)(2,1)S(1)} %bitcast.64), kind=kOutput, calls=%fused_computation.2 | convolution fusion | flops 18874368 | bytes 2146304 | tf_op jit(solution)/shard_map/dot_general | solution.py:71
  (43 shorter events, 2.4 us)
Async XLA Ops:
  7.2 9.5 %copy-start = (bf16[512,1024]{1,0:T(8,128)(2,1)S(1)}, bf16[512,1024]{1,0:T(8,128)(2,1)}, u32[]{:S(2)}) copy-start(bf16[512,1024]{1,0:T(8,128)(2,1)} %param.8) | copy-start | bytes 3145732
  7.2 126.5 %all-gather.6.cloned.1.call-start = ((), (), s32[]{:S(2)}) async-start(), calls=%async_computation.3 | async-start | bytes 17825792 | tf_op jit(solution)/shard_map/all_gather | solution.py:63
  7.9 183.8 %all-gather.8.cloned.1.call-start = ((), (), s32[]{:S(2)}) async-start(), calls=%async_computation.5 | async-start | bytes 4456448 | tf_op jit(solution)/shard_map/all_gather | solution.py:28
  11.4 21.9 %copy-start.2 = (bf16[4,2,8,256]{3,2,0,1:T(8,128)(2,1)}, bf16[4,2,8,256]{3,2,0,1:T(8,128)(2,1)S(1)}, u32[]{:S(2)}) copy-start(bf16[4,2,8,256]{3,2,0,1:T(8,128)(2,1)S(1)} %copy.105) | copy-start | bytes 98308
  16.6 16.6 %copy-start.4 = (bf16[4,2,8,256]{3,2,0,1:T(8,128)(2,1)}, bf16[4,2,8,256]{3,2,0,1:T(8,128)(2,1)S(1)}, u32[]{:S(2)}) copy-start(bf16[4,2,8,256]{3,2,0,1:T(8,128)(2,1)S(1)} %copy.104) | copy-start | bytes 98308
  67.2 175.7 %reduce-scatter.2.cloned.1.call-start = ((), (), s32[]{:S(2)}) async-start(), calls=%async_computation.4 | async-start | bytes 9437184 | tf_op jit(solution)/shard_map/reduce_scatter | solution.py:67
  150.5 0.9 copy-start.1
  150.5 1.3 copy-start.6
  150.5 20.7 %copy-start.7 = (s32[16,4,2]{0,2,1:T(2,128)S(1)}, s32[16,4,2]{0,2,1:T(2,128)}, u32[]{:S(2)}) copy-start(s32[16,4,2]{0,2,1:T(2,128)} %param.14) | copy-start | bytes 1540
  150.5 40.8 %copy-start.5 = (bf16[4,2,8,256]{3,2,0,1:T(8,128)(2,1)S(1)}, bf16[4,2,8,256]{3,2,0,1:T(8,128)(2,1)}, u32[]{:S(2)}) copy-start(bf16[4,2,8,256]{3,2,0,1:T(8,128)(2,1)} %copy-done.4) | copy-start | bytes 98308
  194.9 48.0 %copy-start.3 = (bf16[4,2,8,256]{3,2,0,1:T(8,128)(2,1)S(1)}, bf16[4,2,8,256]{3,2,0,1:T(8,128)(2,1)}, u32[]{:S(2)}) copy-start(bf16[4,2,8,256]{3,2,0,1:T(8,128)(2,1)} %copy-done.2) | copy-start | bytes 98308
Sparse Core Ops, SparseCore 0:
  10.1 123.4 all-gather.5
  136.4 52.7 all-gather.7
  191.5 51.2 reduce-scatter.1
where the time goes:
time: 253 us; the launch traced here: 252 us
  waiting for transfers between devices  98.8 us (39%)
  blocking collectives  82 us (32%)
  matrix products  43.9 us (17%)
  between operations  14 us (6%)
  other arithmetic  8.13 us (3%)
  local copies, waits for them, and re-layouts  5.05 us (2%)
    all_gather x1, waiting for transfers between devices, local(): gathered = lax.all_gather(frozen_weight, 'dp', axis=1, tiled=True)  66.4 us
    all_to_all x2, blocking collectives, from_everyone(): return lax.all_to_all(copies, axis, split_axis=0, concat_axis=0, tiled=True)  45.1 us
    all_gather x2, blocking collectives, gathered_total(): parts = lax.all_gather(x, axis)  36.9 us
    reduce_scatter x1, waiting for transfers between devices, local(): lax.psum_scatter(partial_value, 'tensor', scatter_dimension=1, tiled=True)  31.6 us
    dot_general x1, matrix products, local(): jnp.dot(attn_out, gathered, preferred_element_type=jnp.float32)  16.8 us
    dot_general x1, matrix products, local(): lax.dot_general(out_grad, gathered, (((1,), (1,)), ((), ())), preferred_e...  16.3 us
  transfers between devices with their start and end apart: 3, of which 2 were waited for; matrix products, arithmetic and copies ran while one was open for 21% of the time, Pallas kernels for 0%

commit v1 on v0

--- a/solution.py
+++ b/solution.py
@@ -60,7 +60,9 @@
     back_part = jnp.dot(grad_cols, up_b.T, preferred_element_type=jnp.float32)
     low_total, back_total = packed_total((low_part, back_part), "tensor")
     low_bf = low_total.astype(jnp.bfloat16)
-    gathered = lax.all_gather(frozen_weight, "dp", axis=1, tiled=True)
+    gathered = jnp.concatenate(
+        lax.all_to_all(jnp.stack([frozen_weight] * lax.axis_size("dp")), "dp", 0, 0), axis=1
+    )
     partial_value = jnp.dot(attn_out, gathered, preferred_element_type=jnp.float32).astype(
         jnp.bfloat16
     )

time: 253 us -> 495 us (1.96)
  the two profiles are of different devices: /device:TPU:1 before, /device:TPU:18 now
where the time goes in v1:
time: 495 us; the launch traced here: 494 us
  waiting for transfers between devices  258 us (52%)
  blocking collectives  125 us (25%)
  matrix products  56 us (11%)
  between operations  15.7 us (3%)
  local copies, waits for them, and re-layouts  15.6 us (3%)
  starting transfers between devices  15.1 us (3%)
  other arithmetic  8.23 us (2%)
    all_to_all x1, waiting for transfers between devices, local(): lax.all_to_all(jnp.stack([frozen_weight] * lax.axis_size('dp')), 'dp', 0, 0)  236 us
    all_gather x2, blocking collectives, gathered_total(): parts = lax.all_gather(x, axis)  114 us
    dot_general x1, matrix products, local(): jnp.dot(attn_out, gathered, preferred_element_type=jnp.float32)  29.6 us
    all_to_all x1, waiting for transfers between devices, from_everyone(): return lax.all_to_all(copies, axis, split_axis=0, concat_axis=0, tiled=True)  21.8 us
    dot_general x1, matrix products, local(): lax.dot_general(out_grad, gathered, (((1,), (1,)), ((), ())), preferred_e...  15.6 us
    all_to_all x1, blocking collectives, from_everyone(): return lax.all_to_all(copies, axis, split_axis=0, concat_axis=0, tiled=True)  11.8 us
  transfers between devices with their start and end apart: 4, of which 2 were waited for; matrix products, arithmetic and copies ran while one was open for 11% of the time, Pallas kernels for 0%

profile of v1, /device:TPU:18, one launch (start us, length us, event | category | flops | bytes accessed | tf_op | source)
XLA Modules:
  0.0 494.2 jit_solution(12415607691547703877)
XLA Ops:
  8.0 0.8 rev.7
  8.8 0.7 add_divide_fusion
  9.5 0.8 select_reduce_fusion.2
  10.3 1.2 fusion.2
  11.6 1.6 fusion.4
  13.3 0.7 rev.6
  14.0 0.7 add_divide_fusion.1
  14.7 0.8 select_reduce_fusion.3
  15.5 1.2 fusion.1
  17.8 11.8 %all_to_all.16 = f32[8,1,16384]{2,1,0:T(1,128)S(1)} all-to-all(f32[8,1,16384]{2,1,0:T(1,128)S(1)} %broadcast_in_dim.4), channel_id=1, replica_groups=mesh['dp'=16,'tensor'=8] {'tensor'}, dimensions={0} | all-to-all | bytes 1048576 | tf_op jit(solution)/shard_map/all_to_all | solution.py:11
  29.6 0.5 reduce_sum.101
  30.3 1.5 convolution_multiply_fusion
  31.8 0.4 convolution_bitcast_fusion
  32.5 0.4 fusion
  33.0 1.5 broadcast_in_dim.5
  34.5 6.7 %all-to-all-start.2 = ((f32[8,256,256]{2,1,0:T(8,128)}), f32[8,256,256]{2,1,0:T(8,128)S(1)}, u32[]{:S(2)}, u32[]{:S(2)}) async-start(f32[8,256,256]{2,1,0:T(8,128)} %broadcast_in_dim.5), calls=%async_computation.3 | async-start | bytes 4194304 | tf_op jit(solution)/shard_map/all_to_all | solution.py:11
  41.2 2.3 copy.91
  43.5 21.8 %all-to-all-done.2 = f32[8,256,256]{2,1,0:T(8,128)S(1)} async-done(((f32[8,256,256]{2,1,0:T(8,128)}), f32[8,256,256]{2,1,0:T(8,128)S(1)}, u32[]{:S(2)}, u32[]{:S(2)}) %all-to-all-start.2) | async-done | bytes 2097184 | tf_op jit(solution)/shard_map/all_to_all | solution.py:11
  65.2 6.9 %stack.2 = bf16[16,1024,512]{1,2,0:T(8,128)(2,1)} broadcast(bf16[1024,512]{0,1:T(8,128)(2,1)} %copy.91), dimensions={1,2} | broadcast | bytes 17825792 | tf_op jit(solution)/shard_map/stack | solution.py:64
  72.1 8.3 %all-to-all-start = ((bf16[16,1024,512]{1,2,0:T(8,128)(2,1)}), bf16[16,1024,512]{1,2,0:T(8,128)(2,1)}, u32[]{:S(2)}, u32[]{:S(2)}) async-start(bf16[16,1024,512]{1,2,0:T(8,128)(2,1)} %stack.2), calls=%async_computation | async-start | bytes 33554432 | tf_op jit(solution)/shard_map/all_to_all | solution.py:64
  80.4 0.8 reduce_sum.102
  81.4 236.4 %all-to-all-done = bf16[16,1024,512]{1,2,0:T(8,128)(2,1)} async-done(((bf16[16,1024,512]{1,2,0:T(8,128)(2,1)}), bf16[16,1024,512]{1,2,0:T(8,128)(2,1)}, u32[]{:S(2)}, u32[]{:S(2)}) %all-to-all-start) | async-done | bytes 16777248 | tf_op jit(solution)/shard_map/all_to_all | solution.py:64
  317.7 29.6 %convolution_convert_fusion = bf16[512,8192]{1,0:T(8,128)(2,1)} fusion(bf16[512,1024]{1,0:T(8,128)(2,1)S(1)} %copy-done, bf16[1024,8192]{0,1:T(8,128)(2,1)} %bitcast.1), kind=kOutput, calls=%fused_computation | convolution fusion | flops 8594128896 | bytes 26214400 | tf_op jit(solution)/shard_map/dot_general | solution.py:66
  347.4 0.9 copy-done.2
  349.0 89.4 %all-gather.1 = f32[256,4,2]{1,2,0:T(2,128)S(1)} all-gather(f32[16,4,2]{1,2,0:T(2,128)S(1)} %copy.100), channel_id=3, replica_groups=mesh['dp'=16,'tensor'=8] {'dp'}, dimensions={0}, use_global_device_ids=true | all-gather | bytes 8704 | tf_op jit(solution)/shard_map/all_gather | solution.py:28
  438.5 0.7 copy.103
  439.9 24.1 %all-gather.2 = f32[256,4,2]{1,2,0:T(2,128)S(1)} all-gather(f32[16,4,2]{1,2,0:T(2,128)S(1)} %copy.102), channel_id=4, replica_groups=mesh['dp'=16,'tensor'=8] {'dp'}, dimensions={0}, use_global_device_ids=true | all-gather | bytes 8704 | tf_op jit(solution)/shard_map/all_gather | solution.py:28
  464.1 0.7 copy.104
  464.8 0.4 fusion.23
  465.2 3.3 reduce_sum.103
  468.5 15.6 %add_convert_fusion = bf16[512,1024]{1,0:T(8,128)(2,1)} fusion(f32[512,1024]{1,0:T(8,128)S(1)} %fusion.23, bf16[512,8192]{1,0:T(8,128)(2,1)} %param.15, bf16[1024,8192]{0,1:T(8,128)(2,1)} %bitcast.1), kind=kOutput, calls=%fused_computation.1 | convolution fusion | flops 8591507456 | bytes 28311552 | tf_op jit(solution)/shard_map/dot_general | solution.py:76
  484.2 2.6 add_convert_fusion.1
  (47 shorter events, 3.3 us)
Async XLA Ops:
  8.0 8.8 %copy-start = (bf16[512,1024]{1,0:T(8,128)(2,1)S(1)}, bf16[512,1024]{1,0:T(8,128)(2,1)}, u32[]{:S(2)}) copy-start(bf16[512,1024]{1,0:T(8,128)(2,1)} %param.8) | copy-start | bytes 3145732
  11.5 5.9 %copy-start.3 = (bf16[4,2,8,256]{3,2,0,1:T(8,128)(2,1)}, bf16[4,2,8,256]{3,2,0,1:T(8,128)(2,1)S(1)}, u32[]{:S(2)}) copy-start(bf16[4,2,8,256]{3,2,0,1:T(8,128)(2,1)S(1)} %copy.110) | copy-start | bytes 98308
  16.8 0.7 copy-start.5
  34.5 30.7 %all-to-all-start.2 = ((f32[8,256,256]{2,1,0:T(8,128)}), f32[8,256,256]{2,1,0:T(8,128)S(1)}, u32[]{:S(2)}, u32[]{:S(2)}) async-start(f32[8,256,256]{2,1,0:T(8,128)} %broadcast_in_dim.5), calls=%async_computation.3 | async-start | bytes 4194304 | tf_op jit(solution)/shard_map/all_to_all | solution.py:11
  72.1 245.6 %all-to-all-start = ((bf16[16,1024,512]{1,2,0:T(8,128)(2,1)}), bf16[16,1024,512]{1,2,0:T(8,128)(2,1)}, u32[]{:S(2)}, u32[]{:S(2)}) async-start(bf16[16,1024,512]{1,2,0:T(8,128)(2,1)} %stack.2), calls=%async_computation | async-start | bytes 33554432 | tf_op jit(solution)/shard_map/all_to_all | solution.py:64
  80.4 384.9 %all-gather.5.cloned.1.call-start = ((), (), s32[]{:S(2)}) async-start(), calls=%async_computation.5 | async-start | bytes 4456448 | tf_op jit(solution)/shard_map/all_gather | solution.py:28
  81.3 402.9 %reduce-scatter.2.cloned.1.call-start = ((), (), s32[]{:S(2)}) async-start(), calls=%async_computation.4 | async-start | bytes 9437184 | tf_op jit(solution)/shard_map/reduce_scatter | solution.py:69
  347.3 0.9 copy-start.2
  347.3 1.3 copy-start.7
  347.3 92.2 %copy-start.8 = (s32[16,4,2]{0,2,1:T(2,128)S(1)}, s32[16,4,2]{0,2,1:T(2,128)}, u32[]{:S(2)}) copy-start(s32[16,4,2]{0,2,1:T(2,128)} %param.14) | copy-start | bytes 1540
  347.3 117.5 %copy-start.6 = (bf16[4,2,8,256]{3,2,0,1:T(8,128)(2,1)S(1)}, bf16[4,2,8,256]{3,2,0,1:T(8,128)(2,1)}, u32[]{:S(2)}) copy-start(bf16[4,2,8,256]{3,2,0,1:T(8,128)(2,1)} %copy-done.5) | copy-start | bytes 98308
  468.5 15.6 %copy-start.4 = (bf16[4,2,8,256]{3,2,0,1:T(8,128)(2,1)S(1)}, bf16[4,2,8,256]{3,2,0,1:T(8,128)(2,1)}, u32[]{:S(2)}) copy-start(bf16[4,2,8,256]{3,2,0,1:T(8,128)(2,1)} %copy-done.3) | copy-start | bytes 98308
  468.5 18.3 %copy-start.1 = (bf16[512,1024]{1,0:T(8,128)(2,1)S(1)}, bf16[512,1024]{1,0:T(8,128)(2,1)}, u32[]{:S(2)}) copy-start(bf16[512,1024]{1,0:T(8,128)(2,1)} %param.8) | copy-start | bytes 3145732
Sparse Core Ops, SparseCore 0:
  83.9 243.9 all-gather.4
Sparse Core Ops, SparseCore 1:
  347.5 118.7 reduce-scatter.1
